TPU v7x, 1024 devices: a whole 8x8x8 slice. The times are simulated.
1024 devices in a mesh: ctx: 16 (over y, z_lo), section: 8 (over x), tp: 8 (over z_hi, core).
Axes of the slice: x: 8, y: 8, z: 8 (z_hi: 4, z_lo: 2; z = z_hi * 2 + z_lo), core: 2. Of those that a mesh axis runs over, the one named last changes fastest.
Arguments:
- row_offsets: int32 [8], P('section'), may hold values from 7552 to 8192
- queries: bfloat16 [8, 2048, 4096], P('section', 'ctx', 'tp'), may hold values from -8 to 8
- cache_keys: bfloat16 [8, 10240, 1024], P('section', 'ctx', 'tp'), may hold values from -4 to 4
- cache_values: bfloat16 [8, 10240, 1024], P('section', 'ctx', 'tp'), may hold values from -6 to 6
- residual: bfloat16 [8, 2048, 5120], P('section', 'ctx', 'tp'), may hold values from -6 to 6
- out_weight: bfloat16 [8, 4096, 5120], P('section', 'tp'), may hold values from -0.09375 to 0.09375
Outputs:
- next_inputs: bfloat16 [8, 2048, 5120], P('section', 'ctx', 'tp')
All inputs are finite; a program needn't handle non-finite values.
Results may differ from a plain program's by a relative error of at most 0.0085.
Values may be sent and summed in bfloat16 or wider, within the bound.
A program may use at most 32 MiB of HBM per device.

v0:
```python
import functools

import jax
import jax.numpy as jnp
from jax import lax
from jax.experimental import pallas as pl
from jax.experimental.pallas import tpu as pltpu
from jax.sharding import PartitionSpec as P

HD = 128
G = 4
NEG = -(2.0**100)
LOG2E = 1.4426950408889634
AHEAD = 3
PARTS = 2
MESH = pl.DeviceIdType.MESH
BF = jnp.bfloat16
F32 = jnp.float32


def kernel(
    ny, nzh, nx,
    off_ref, q_ref, k_ref, v_ref, res_ref, w_ref, o_ref,
    kbuf, vbuf, vt, qb, snd, rcv, att, wbuf, keep, base,
    far_s, far_r, near_s, near_r, mix_s, mix_r, fin,
    kv_l, kv_s, kv_r, q_l, q_s, q_r, a_s, a_r, w_l, w_s, w_r, t_s, t_r,
    far_ss, far_rs, near_ss, near_rs, mix_ss, mix_rs, x_s, x_r,
):
    rows = q_ref.shape[0]
    klen = k_ref.shape[0]
    width = res_ref.shape[1]
    half = rows // 2
    part = half // PARTS
    two = 2 * HD

    ctx = lax.axis_index("ctx")
    tp = lax.axis_index("tp")
    x = lax.axis_index("section")
    y, zl = ctx // 2, ctx % 2
    zh, co = tp // 2, tp % 2
    y_next = {"ctx": ((y + 1) % ny) * 2 + zl}
    y_prev = {"ctx": ((y + ny - 1) % ny) * 2 + zl}
    ring = (y_next, y_prev)
    z_mate = {"ctx": y * 2 + 1 - zl}
    core_mate = {"tp": zh * 2 + 1 - co}
    zh_next = {"tp": ((zh + 1) % nzh) * 2 + co}
    zh_prev = {"tp": ((zh + nzh - 1) % nzh) * 2 + co}
    zring = (zh_next, zh_prev)
    x_next = {"section": (x + 1) % nx}
    x_prev = {"section": (x + nx - 1) % nx}

    def remote(src, dst, s, r, where):
        return pltpu.make_async_remote_copy(
            src_ref=src, dst_ref=dst, send_sem=s, recv_sem=r, device_id=where, device_id_type=MESH
        )

    def wcols(block, core):
        return pl.ds(pl.multiple_of(block * 2 * width + core * width, width), width)

    own_rows = pl.ds(pl.multiple_of(zl * klen, klen), klen)
    local_k = pltpu.make_async_copy(k_ref, kbuf.at[own_rows], kv_l.at[0])
    local_v = pltpu.make_async_copy(v_ref, vbuf.at[own_rows], kv_l.at[1])
    local_q = [
        pltpu.make_async_copy(q_ref.at[:, pl.ds(d * two, two)], qb.at[d, ny - 1], q_l.at[d]) for d in (0, 1)
    ]
    local_w = [
        pltpu.make_async_copy(w_ref.at[:, wcols(b, co)], wbuf.at[b, co], w_l.at[b]) for b in range(nzh)
    ]
    local_k.start()
    local_v.start()
    for c in local_q:
        c.start()

    barrier = pltpu.get_barrier_semaphore()
    greet = (y_next, y_prev, z_mate, core_mate, zh_next, zh_prev, x_next, x_prev)
    for where in greet:
        pl.semaphore_signal(barrier, inc=1, device_id=where, device_id_type=MESH)
    pl.semaphore_wait(barrier, len(greet))

    send_k = remote(k_ref, kbuf.at[own_rows], kv_s.at[0], kv_r.at[0], z_mate)
    send_v = remote(v_ref, vbuf.at[own_rows], kv_s.at[1], kv_r.at[1], z_mate)
    send_k.start()
    send_v.start()
    for d in (0, 1):
        remote(
            q_ref.at[:, pl.ds(d * two, two)], qb.at[d, 0], q_s.at[d, 0], q_r.at[d, 0], ring[d]
        ).start()

    def q_hop(d, slot):
        return remote(qb.at[d, slot], qb.at[d, slot + 1], q_s.at[d, slot + 1], q_r.at[d, slot + 1], ring[d])

    def q_arrival(d, slot):
        return remote(qb.at[d, slot], qb.at[d, slot], q_s.at[d, slot], q_r.at[d, slot], ring[d])

    send_w = [
        remote(w_ref.at[:, wcols(b, 1 - co)], wbuf.at[b, co], w_s.at[b], w_r.at[b], core_mate)
        for b in range(nzh)
    ]
    for c in local_w:
        c.start()
    for c in send_w:
        c.start()

    lane_row = lax.broadcasted_iota(jnp.int32, (1, two), 1) % rows
    key_pos = y * (2 * klen) + lax.broadcasted_iota(jnp.int32, (2 * klen, two), 0)
    offset = off_ref[0]
    stat_row = lax.broadcasted_iota(jnp.int32, (16, HD), 0)
    scale = HD ** (-0.5) * LOG2E

    for d in (0, 1):
        for h in (0, 1):
            rcv[d, 0, h, 0:HD, :] = jnp.zeros((HD, HD), BF)
            rcv[d, 0, h, HD:, :] = jnp.where(stat_row == 0, NEG, 0.0).astype(BF)

    for slot in range(AHEAD):
        for d in (0, 1):
            q_arrival(d, slot).wait_recv()
            q_hop(d, slot).start()
    for c in local_q:
        c.wait()
    local_k.wait()
    local_v.wait()
    send_k.wait_recv()
    send_v.wait_recv()
    vt[...] = vbuf[...].T

    def acc_hop(d, t, h):
        return remote(snd.at[d, t, h], rcv.at[d, t + 1, h], a_s.at[d, t, h], a_r.at[d, t + 1, h], ring[d])

    def acc_arrival(d, t, h):
        return remote(snd.at[d, t, h], rcv.at[d, t, h], a_s.at[d, t, h], a_r.at[d, t, h], ring[d])

    def advance(t, carry):
        for d in (0, 1):
            ahead = t + AHEAD

            @pl.when(ahead < ny - 1)
            def _():
                q_arrival(d, ahead).wait_recv()

            @pl.when(ahead < ny - 2)
            def _():
                q_hop(d, ahead).start()

        for d in (0, 1):
            block = (y + 2 * ny - 1 - t) % ny if d == 0 else (y + 1 + t) % ny
            q2 = qb[d, t]
            q2 = jnp.concatenate([q2[:, :HD], q2[:, HD:]], axis=0)
            scores = lax.dot_general(
                kbuf[...], q2, (((1,), (1,)), ((), ())), preferred_element_type=F32
            )
            row_pos = offset + (block * 2 + zl) * rows + lane_row
            scores = jnp.where(key_pos <= row_pos, scores, NEG)
            top = jnp.max(scores, axis=0, keepdims=True).astype(BF).astype(F32)
            weights = jnp.exp2((scores - top) * scale)
            total = jnp.sum(weights, axis=0, keepdims=True)
            mixed = jnp.dot(vt[...], weights.astype(BF), preferred_element_type=F32)
            for h in (0, 1):
                cols = slice(h * HD, (h + 1) * HD)

                @pl.when(t > 0)
                def _():
                    acc_arrival(d, t, h).wait_recv()

                stats = rcv[d, t, h, HD:, :].astype(F32)
                top_in = stats[0:1]
                sum_in = stats[1:2] + stats[2:3]
                top_new = jnp.maximum(top_in, top[:, cols])
                f_in = jnp.exp2((top_in - top_new) * scale)
                f_own = jnp.exp2((top[:, cols] - top_new) * scale)
                sum_new = sum_in * f_in + total[:, cols] * f_own
                acc_new = rcv[d, t, h, 0:HD, :].astype(F32) * f_in + mixed[:, cols] * f_own

                @pl.when(t < ny - 1)
                def _():
                    snd[d, t, h, 0:HD, :] = acc_new.astype(BF)
                    high = sum_new.astype(BF).astype(F32)
                    packed = jnp.where(
                        stat_row == 0,
                        top_new,
                        jnp.where(stat_row == 1, high, jnp.where(stat_row == 2, sum_new - high, 0.0)),
                    )
                    snd[d, t, h, HD:, :] = packed.astype(BF)
                    acc_hop(d, t, h).start()

                @pl.when(t == ny - 1)
                def _():
                    head = (acc_new / sum_new).T
                    att[co, :, (2 * d + h) * HD : (2 * d + h + 1) * HD] = head.astype(BF)

        return carry

    lax.fori_loop(0, ny, advance, 0)

    send_t = remote(att.at[co], att.at[co], t_s, t_r, core_mate)
    send_t.start()
    for c in local_w:
        c.wait()
    for c in send_w:
        c.wait_recv()
    send_t.wait_recv()

    def product(away):
        dest = (zh + away) % nzh
        out = jnp.dot(att[0], wbuf[dest, 0], preferred_element_type=F32)
        return out + jnp.dot(att[1], wbuf[dest, 1], preferred_element_type=F32)

    def span(i, j):
        return slice(i * half + j * part, i * half + (j + 1) * part)

    far_cp = [[remote(far_s.at[i, j], far_r.at[i, j], far_ss.at[i, j], far_rs.at[i, j], zring[i]) for j in range(PARTS)] for i in (0, 1)]
    near_cp = [[remote(near_s.at[i, j], near_r.at[i, j], near_ss.at[i, j], near_rs.at[i, j], zring[i]) for j in range(PARTS)] for i in (0, 1)]
    mix_cp = [[remote(mix_s.at[i, j], mix_r.at[i, j], mix_ss.at[i, j], mix_rs.at[i, j], zring[i]) for j in range(PARTS)] for i in (0, 1)]
    fin_cp = [
        [remote(fin.at[span(i, j)], o_ref.at[span(i, j)], x_s.at[i, j], x_r.at[i, j], x_next) for j in range(PARTS)]
        for i in (0, 1)
    ]

    opposite = product(2)
    for j in range(PARTS):
        for i in (0, 1):
            far_s[i, j] = opposite[span(i, j)].astype(BF)
            far_cp[i][j].start()
    for i in (0, 1):
        out = product(1 if i == 0 else nzh - 1)
        keep[i] = out[i * half : (i + 1) * half]
        for j in range(PARTS):
            near_s[i, j] = out[span(1 - i, j)].astype(BF)
            near_cp[i][j].start()
    base[...] = product(0) + res_ref[...].astype(F32)
    for j in range(PARTS):
        for i in (0, 1):
            far_cp[i][j].wait_recv()
            mix_s[i, j] = (keep[i, j * part : (j + 1) * part] + far_r[i, j].astype(F32)).astype(BF)
            mix_cp[i][j].start()
    for j in range(PARTS):
        for i in (0, 1):
            near_cp[1 - i][j].wait_recv()
            mix_cp[i][j].wait_recv()
            summed = base[span(i, j)] + near_r[1 - i, j].astype(F32) + mix_r[i, j].astype(F32)
            fin[span(i, j)] = summed.astype(BF)
            fin_cp[i][j].start()

    send_k.wait_send()
    send_v.wait_send()
    for c in send_w:
        c.wait_send()
    send_t.wait_send()

    def drain_q(s, carry):
        for d in (0, 1):
            q_arrival(d, s).wait_send()
            for h in (0, 1):
                acc_hop(d, s, h).wait_send()
        return carry

    lax.fori_loop(0, ny - 1, drain_q, 0)
    for i in (0, 1):
        for j in range(PARTS):
            far_cp[i][j].wait_send()
            near_cp[i][j].wait_send()
            mix_cp[i][j].wait_send()
    for i in (0, 1):
        for j in range(PARTS):
            fin_cp[i][j].wait_send()
            fin_cp[i][j].wait_recv()


def on_device(ny, nzh, nx, row_offsets, queries, cache_keys, cache_values, residual, out_weight):
    q, k, v, res, w = queries[0], cache_keys[0], cache_values[0], residual[0], out_weight[0]
    rows, klen, width = q.shape[0], k.shape[0], res.shape[1]
    half = rows // 2
    part = half // PARTS
    dma = pltpu.SemaphoreType.DMA
    piece = pltpu.VMEM((2, PARTS, part, width), BF)
    any_spec = pl.BlockSpec(memory_space=pl.ANY)
    out = pl.pallas_call(
        functools.partial(kernel, ny, nzh, nx),
        out_shape=jax.ShapeDtypeStruct(res.shape, BF),
        in_specs=[
            pl.BlockSpec(memory_space=pltpu.SMEM),
            any_spec, any_spec, any_spec,
            pl.BlockSpec(memory_space=pltpu.VMEM),
            any_spec,
        ],
        out_specs=any_spec,
        scratch_shapes=[
            pltpu.VMEM((2 * klen, HD), BF),
            pltpu.VMEM((2 * klen, HD), BF),
            pltpu.VMEM((HD, 2 * klen), BF),
            pltpu.VMEM((2, ny, rows, 2 * HD), BF),
            pltpu.VMEM((2, ny, 2, HD + 16, HD), BF),
            pltpu.VMEM((2, ny, 2, HD + 16, HD), BF),
            pltpu.VMEM((2, rows, G * HD), BF),
            pltpu.VMEM((nzh, 2, w.shape[0], width), BF),
            pltpu.VMEM((2, half, width), F32),
            pltpu.VMEM((rows, width), F32),
            piece, piece, piece, piece, piece, piece,
            pltpu.VMEM((rows, width), BF),
            dma((2,)), dma((2,)), dma((2,)),
            dma((2,)), dma((2, ny)), dma((2, ny)),
            dma((2, ny, 2)), dma((2, ny, 2)),
            dma((nzh,)), dma((nzh,)), dma((nzh,)),
            dma(()), dma(()),
            dma((2, PARTS)), dma((2, PARTS)), dma((2, PARTS)), dma((2, PARTS)), dma((2, PARTS)), dma((2, PARTS)),
            dma((2, PARTS)), dma((2, PARTS)),
        ],
        compiler_params=pltpu.CompilerParams(
            collective_id=0, has_side_effects=True, vmem_limit_bytes=48 * 1024 * 1024
        ),
    )(row_offsets, q, k, v, res, w)
    return out[None]


def solution(mesh):
    placed = (
        P("section"),
        P("section", "ctx", "tp"),
        P("section", "ctx", "tp"),
        P("section", "ctx", "tp"),
        P("section", "ctx", "tp"),
        P("section", "tp", None),
    )
    ny, nzh, nx = mesh.shape["ctx"] // 2, mesh.shape["tp"] // 2, mesh.shape["section"]
    return jax.shard_map(
        functools.partial(on_device, ny, nzh, nx),
        mesh=mesh, in_specs=placed, out_specs=P("section", "ctx", "tp"), check_vma=False,
    )
```

profile of v0, /device:TPU:1, one launch (start us, length us, event | category | flops | bytes accessed | tf_op | source)
XLA Modules:
  0.0 90.2 jit_solution(658812101054362513)
XLA Ops:
  0.7 0.0 copy-start
  0.7 2.5 %copy-done = bf16[1,512,5120]{2,1,0:T(8,128)(2,1)S(1)} copy-done((bf16[1,512,5120]{2,1,0:T(8,128)(2,1)S(1)}, bf16[1,512,5120]{2,1,0:T(8,128)(2,1)}, u32[]{:S(2)}) %copy-start) | copy-done | bytes 5242904
  3.1 0.0 copy-start.1
  3.1 0.9 %copy-done.1 = bf16[1,640,128]{2,1,0:T(8,128)(2,1)S(1)} copy-done((bf16[1,640,128]{2,1,0:T(8,128)(2,1)S(1)}, bf16[1,640,128]{2,1,0:T(8,128)(2,1)}, u32[]{:S(2)}) %copy-start.1) | copy-done | bytes 163864
  4.1 0.0 copy-start.2
  4.1 0.9 %copy-done.2 = bf16[1,640,128]{2,1,0:T(8,128)(2,1)S(1)} copy-done((bf16[1,640,128]{2,1,0:T(8,128)(2,1)S(1)}, bf16[1,640,128]{2,1,0:T(8,128)(2,1)}, u32[]{:S(2)}) %copy-start.2) | copy-done | bytes 163864
  5.0 0.0 copy-start.3
  5.0 0.9 %copy-done.3 = bf16[1,128,640]{2,1,0:T(8,128)(2,1)S(1)} copy-done((bf16[1,128,640]{2,1,0:T(8,128)(2,1)S(1)}, bf16[1,128,640]{2,1,0:T(8,128)(2,1)}, u32[]{:S(2)}) %copy-start.3) | copy-done | bytes 163864
  5.9 0.0 copy-start.4
  5.9 0.9 %copy-done.4 = bf16[1,128,512]{2,1,0:T(8,128)(2,1)S(1)} copy-done((bf16[1,128,512]{2,1,0:T(8,128)(2,1)S(1)}, bf16[1,128,512]{2,1,0:T(8,128)(2,1)}, u32[]{:S(2)}) %copy-start.4) | copy-done | bytes 131096
  6.8 82.7 %shard_map.64 = bf16[128,640]{1,0:T(8,128)(2,1)S(1)} custom-call(s32[1]{0:T(128)S(6)} %copy.8.off_ref, bf16[128,512]{1,0:T(8,128)(2,1)S(1)} %bitcast.11, bf16[640,128]{1,0:T(8,128)(2,1)S(1)} %bitcast.8, bf16[640,128]{1,0:T(8,128)(2,1)S(1)} %bitcast.9, bf16[128,640]{1,0:T(8,128)(2,1)S(1)} %bitcast.10, bf16[512,5120]{1,0:T(8,128)(2,1)S(1)} %bitcast.6), custom_call_target="tpu_custom_call" | custom-call | tf_op jit(solution)/shard_map/pallas_call | solution.py:277
  89.5 0.7 copy.9
Async XLA Ops:
  0.7 2.5 %copy-start = (bf16[1,512,5120]{2,1,0:T(8,128)(2,1)S(1)}, bf16[1,512,5120]{2,1,0:T(8,128)(2,1)}, u32[]{:S(2)}) copy-start(bf16[1,512,5120]{2,1,0:T(8,128)(2,1)} %param.11) | copy-start | bytes 15728644
  3.1 0.9 %copy-start.1 = (bf16[1,640,128]{2,1,0:T(8,128)(2,1)S(1)}, bf16[1,640,128]{2,1,0:T(8,128)(2,1)}, u32[]{:S(2)}) copy-start(bf16[1,640,128]{2,1,0:T(8,128)(2,1)} %param.8) | copy-start | bytes 491524
  4.1 0.9 %copy-start.2 = (bf16[1,640,128]{2,1,0:T(8,128)(2,1)S(1)}, bf16[1,640,128]{2,1,0:T(8,128)(2,1)}, u32[]{:S(2)}) copy-start(bf16[1,640,128]{2,1,0:T(8,128)(2,1)} %param.9) | copy-start | bytes 491524
  5.0 0.9 %copy-start.3 = (bf16[1,128,640]{2,1,0:T(8,128)(2,1)S(1)}, bf16[1,128,640]{2,1,0:T(8,128)(2,1)}, u32[]{:S(2)}) copy-start(bf16[1,128,640]{2,1,0:T(8,128)(2,1)} %param.10) | copy-start | bytes 491524
  5.9 0.9 %copy-start.4 = (bf16[1,128,512]{2,1,0:T(8,128)(2,1)S(1)}, bf16[1,128,512]{2,1,0:T(8,128)(2,1)}, u32[]{:S(2)}) copy-start(bf16[1,128,512]{2,1,0:T(8,128)(2,1)} %param.7) | copy-start | bytes 393220
where the time goes:
time: 90.5 us; the launch traced here: 90.2 us
  Pallas kernels  82.7 us (91%)
  local copies, waits for them, and re-layouts  6.8 us (8%)
    pallas_call x1, Pallas kernels, on_device(): pl.pallas_call(functools.partial(kernel, ny, nzh, nx), out_shape=jax.Shap...  82.7 us
    unnamed x11, local copies, waits for them, and re-layouts  6.8 us

commit v1 on v0

v1 whole, which is shorter than its diff:
```python
import functools

import jax
import jax.numpy as jnp
from jax import lax
from jax.experimental import pallas as pl
from jax.experimental.pallas import tpu as pltpu
from jax.sharding import PartitionSpec as P

HD = 128
G = 4
NEG = -(2.0**100)
LOG2E = 1.4426950408889634
PARTS = 2
MESH = pl.DeviceIdType.MESH
BF = jnp.bfloat16
F32 = jnp.float32


def kernel(
    ny, nzh, nx,
    off_ref, q_ref, k_ref, v_ref, res_ref, w_ref, o_ref,
    kb, vb, qin, qs, m_ref, l_ref, acc, snd, rcv, att, wbuf, resv, keep, base,
    far_s, far_r, near_s, near_r, mix_s, mix_r, fin,
    loc, kv_s, kv_r, q_s, q_r, a_s, a_r, w_l, w_s, w_r, t_s, t_r,
    far_ss, far_rs, near_ss, near_rs, mix_ss, mix_rs, x_s, x_r,
):
    rows = q_ref.shape[0]
    klen = k_ref.shape[0]
    width = res_ref.shape[1]
    half = rows // 2
    part = half // PARTS
    two = 2 * HD
    hops = ny // 2
    cut = (klen // HD + 1) // 2 * HD
    spans = ((0, cut), (cut, klen - cut))

    ctx = lax.axis_index("ctx")
    tp = lax.axis_index("tp")
    x = lax.axis_index("section")
    y, zl = ctx // 2, ctx % 2
    zh, co = tp // 2, tp % 2
    y_next = {"ctx": ((y + 1) % ny) * 2 + zl}
    y_prev = {"ctx": ((y + ny - 1) % ny) * 2 + zl}
    ring = (y_next, y_prev)
    z_mate = {"ctx": y * 2 + 1 - zl}
    core_mate = {"tp": zh * 2 + 1 - co}
    zh_next = {"tp": ((zh + 1) % nzh) * 2 + co}
    zh_prev = {"tp": ((zh + nzh - 1) % nzh) * 2 + co}
    zring = (zh_next, zh_prev)
    x_next = {"section": (x + 1) % nx}
    x_prev = {"section": (x + nx - 1) % nx}

    def remote(src, dst, s, r, where):
        return pltpu.make_async_remote_copy(
            src_ref=src, dst_ref=dst, send_sem=s, recv_sem=r, device_id=where, device_id_type=MESH
        )

    def wcols(block, core):
        return pl.ds(pl.multiple_of(block * 2 * width + core * width, width), width)

    local_k = pltpu.make_async_copy(k_ref, kb.at[0], loc.at[0])
    local_v = pltpu.make_async_copy(v_ref, vb.at[0], loc.at[1])
    local_q = pltpu.make_async_copy(q_ref, qin.at[0], loc.at[2])
    local_r = pltpu.make_async_copy(res_ref, resv, loc.at[3])
    local_w = [
        pltpu.make_async_copy(w_ref.at[:, wcols(b, co)], wbuf.at[b, co], w_l.at[b]) for b in range(nzh)
    ]
    local_q.start()
    local_k.start()
    local_v.start()

    barrier = pltpu.get_barrier_semaphore()
    greet = (y_next, y_prev, z_mate, core_mate, zh_next, zh_prev, x_next, x_prev)
    for where in greet:
        pl.semaphore_signal(barrier, inc=1, device_id=where, device_id_type=MESH)
    pl.semaphore_wait(barrier, len(greet))

    def hop(src, slot, i, way, kind):
        at = pl.ds(*spans[i])
        dst = (kb, vb)[kind].at[slot, at]
        return remote(src.at[at], dst, kv_s.at[slot, i, kind], kv_r.at[slot, i, kind], ring[way])

    send_q = remote(q_ref, qin.at[1], q_s, q_r, z_mate)
    for i in (0, 1):
        for kind in (0, 1):
            for way in (0, 1):
                hop((k_ref, v_ref)[kind], 1 + way, i, way, kind).start()
        if i == 0:
            send_q.start()
    send_w = [
        remote(w_ref.at[:, wcols(b, 1 - co)], wbuf.at[b, co], w_s.at[b], w_r.at[b], core_mate)
        for b in range(nzh)
    ]
    for c in send_w:
        c.start()
    for c in local_w:
        c.start()
    local_r.start()

    m_ref[...] = jnp.full(m_ref.shape, NEG, F32)
    l_ref[...] = jnp.zeros(l_ref.shape, F32)
    acc[...] = jnp.zeros(acc.shape, F32)
    lane_row = lax.broadcasted_iota(jnp.int32, (1, two), 1) % rows
    offset = off_ref[0]
    stat_row = lax.broadcasted_iota(jnp.int32, (16, two), 0)
    scale = HD ** (-0.5) * LOG2E

    def lay_queries(c):
        for g in (0, 1):
            for h in (0, 1):
                col = (2 * g + h) * HD
                qs[2 * c + g, h * rows : (h + 1) * rows, :] = qin[c, :, col : col + HD]

    def attend(slot, block, i, first, last):
        start, size = spans[i]

        def group(g, carry):
            other = g // 2
            row_pos = offset + (y * 2 + zl + other * (1 - 2 * zl)) * rows + lane_row
            key_pos = (block * 2 + zl) * klen + start + lax.broadcasted_iota(jnp.int32, (size, two), 0)
            scores = lax.dot_general(
                kb[slot, start : start + size, :],
                qs[g],
                (((1,), (1,)), ((), ())),
                preferred_element_type=F32,
            )
            scores = jnp.where(key_pos <= row_pos, scores, NEG)
            top = jnp.max(scores, axis=0, keepdims=True).astype(BF).astype(F32)
            top_old = m_ref[g]
            top = jnp.maximum(top, top_old)
            weights = jnp.exp2((scores - top) * scale)
            fade = jnp.exp2((top_old - top) * scale)
            m_ref[g] = top
            l_ref[g] = l_ref[g] * fade + jnp.sum(weights, axis=0, keepdims=True)
            mixed = lax.dot_general(
                vb[slot, start : start + size, :],
                weights.astype(BF),
                (((0,), (0,)), ((), ())),
                preferred_element_type=F32,
            )
            acc[g] = acc[g] * fade + mixed
            return carry

        lax.fori_loop(first, last, group, 0)

    def arrive(slot, i, way, kind):
        return hop((kb, vb)[kind].at[slot], slot, i, way, kind)

    local_q.wait()
    lay_queries(0)
    local_k.wait()
    local_v.wait()
    for i in (0, 1):
        attend(0, y, i, 0, 2)

    def round_trip(h, carry):
        for i in (0, 1):
            for kind in (0, 1):
                for way in (0, 1):
                    slot = 2 * h - 1 + way
                    arrive(slot, i, way, kind).wait_recv()
                    dest = 2 * h + 1 if way == 0 else jnp.minimum(2 * h + 2, ny - 1)
                    onward = hop((kb, vb)[kind].at[slot], dest, i, way, kind)
                    if way == i:
                        onward.start()
                    else:

                        @pl.when(h < hops - 1)
                        def _():
                            onward.start()

            if i == 0:

                @pl.when(h == 1)
                def _():
                    send_q.wait_recv()
                    lay_queries(1)
                    for j in (0, 1):
                        attend(0, y, j, 2, 4)

            def each(way, c):
                block = (y + ny + way * 2 * h - h) % ny
                attend(2 * h - 1 + way, block, i, 0, 4)
                return c

            lax.fori_loop(0, 2, each, 0)
        return carry

    lax.fori_loop(1, hops, round_trip, 0)

    last = ny - 1
    far_block = (y + hops) % ny
    for kind in (0, 1):
        arrive(last, 0, 0, kind).wait_recv()
    attend(last, far_block, 0, 0, 4)
    for kind in (0, 1):
        arrive(last, 1, 1, kind).wait_recv()
    attend(last, far_block, 1, 2, 4)
    send_a = [remote(snd.at[g], rcv.at[g], a_s.at[g], a_r.at[g], z_mate) for g in (0, 1)]
    for g in (0, 1):
        snd[g, 0:HD, :] = acc[2 + g].astype(BF)
        total = l_ref[2 + g]
        high = total.astype(BF).astype(F32)
        packed = jnp.where(
            stat_row == 0,
            m_ref[2 + g],
            jnp.where(stat_row == 1, high, jnp.where(stat_row == 2, total - high, 0.0)),
        )
        snd[g, HD:, :] = packed.astype(BF)
        send_a[g].start()
    attend(last, far_block, 1, 0, 2)
    for g in (0, 1):
        send_a[g].wait_recv()
        stats = rcv[g, HD:, :].astype(F32)
        top_in = stats[0:1]
        sum_in = stats[1:2] + stats[2:3]
        top_new = jnp.maximum(top_in, m_ref[g])
        f_in = jnp.exp2((top_in - top_new) * scale)
        f_own = jnp.exp2((m_ref[g] - top_new) * scale)
        sum_new = sum_in * f_in + l_ref[g] * f_own
        head = (rcv[g, 0:HD, :].astype(F32) * f_in + acc[g] * f_own) / sum_new
        for h in (0, 1):
            col = (2 * g + h) * HD
            att[co, :, col : col + HD] = head[:, h * rows : (h + 1) * rows].T.astype(BF)

    send_t = remote(att.at[co], att.at[co], t_s, t_r, core_mate)
    send_t.start()
    for c in local_w:
        c.wait()
    for c in send_w:
        c.wait_recv()
    local_r.wait()
    send_t.wait_recv()

    def product(away):
        dest = (zh + away) % nzh
        out = jnp.dot(att[0], wbuf[dest, 0], preferred_element_type=F32)
        return out + jnp.dot(att[1], wbuf[dest, 1], preferred_element_type=F32)

    def span(i, j):
        return slice(i * half + j * part, i * half + (j + 1) * part)

    far_cp = [[remote(far_s.at[i, j], far_r.at[i, j], far_ss.at[i, j], far_rs.at[i, j], zring[i]) for j in range(PARTS)] for i in (0, 1)]
    near_cp = [[remote(near_s.at[i, j], near_r.at[i, j], near_ss.at[i, j], near_rs.at[i, j], zring[i]) for j in range(PARTS)] for i in (0, 1)]
    mix_cp = [[remote(mix_s.at[i, j], mix_r.at[i, j], mix_ss.at[i, j], mix_rs.at[i, j], zring[i]) for j in range(PARTS)] for i in (0, 1)]
    fin_cp = [
        [remote(fin.at[span(i, j)], o_ref.at[span(i, j)], x_s.at[i, j], x_r.at[i, j], x_next) for j in range(PARTS)]
        for i in (0, 1)
    ]

    opposite = product(2)
    for j in range(PARTS):
        for i in (0, 1):
            far_s[i, j] = opposite[span(i, j)].astype(BF)
            far_cp[i][j].start()
    for i in (0, 1):
        out = product(1 if i == 0 else nzh - 1)
        keep[i] = out[i * half : (i + 1) * half]
        for j in range(PARTS):
            near_s[i, j] = out[span(1 - i, j)].astype(BF)
            near_cp[i][j].start()
    base[...] = product(0) + resv[...].astype(F32)
    for j in range(PARTS):
        for i in (0, 1):
            far_cp[i][j].wait_recv()
            mix_s[i, j] = (keep[i, j * part : (j + 1) * part] + far_r[i, j].astype(F32)).astype(BF)
            mix_cp[i][j].start()
    for j in range(PARTS):
        for i in (0, 1):
            near_cp[1 - i][j].wait_recv()
            mix_cp[i][j].wait_recv()
            summed = base[span(i, j)] + near_r[1 - i, j].astype(F32) + mix_r[i, j].astype(F32)
            fin[span(i, j)] = summed.astype(BF)
            fin_cp[i][j].start()

    send_q.wait_send()
    for c in send_w:
        c.wait_send()
    send_t.wait_send()
    for c in send_a:
        c.wait_send()

    def drain(slot, carry):
        for i in (0, 1):
            for kind in (0, 1):
                arrive(slot, i, 0, kind).wait_send()
        return carry

    lax.fori_loop(1, ny, drain, 0)
    for i in (0, 1):
        for j in range(PARTS):
            far_cp[i][j].wait_send()
            near_cp[i][j].wait_send()
            mix_cp[i][j].wait_send()
    for i in (0, 1):
        for j in range(PARTS):
            fin_cp[i][j].wait_send()
            fin_cp[i][j].wait_recv()


def on_device(ny, nzh, nx, row_offsets, queries, cache_keys, cache_values, residual, out_weight):
    q, k, v, res, w = queries[0], cache_keys[0], cache_values[0], residual[0], out_weight[0]
    rows, klen, width = q.shape[0], k.shape[0], res.shape[1]
    half = rows // 2
    part = half // PARTS
    dma = pltpu.SemaphoreType.DMA
    piece = pltpu.VMEM((2, PARTS, part, width), BF)
    any_spec = pl.BlockSpec(memory_space=pl.ANY)
    out = pl.pallas_call(
        functools.partial(kernel, ny, nzh, nx),
        out_shape=jax.ShapeDtypeStruct(res.shape, BF),
        in_specs=[pl.BlockSpec(memory_space=pltpu.SMEM)] + [any_spec] * 5,
        out_specs=any_spec,
        scratch_shapes=[
            pltpu.VMEM((ny, klen, HD), BF),
            pltpu.VMEM((ny, klen, HD), BF),
            pltpu.VMEM((2, rows, G * HD), BF),
            pltpu.VMEM((4, 2 * rows, HD), BF),
            pltpu.VMEM((4, 1, 2 * HD), F32),
            pltpu.VMEM((4, 1, 2 * HD), F32),
            pltpu.VMEM((4, HD, 2 * HD), F32),
            pltpu.VMEM((2, HD + 16, 2 * HD), BF),
            pltpu.VMEM((2, HD + 16, 2 * HD), BF),
            pltpu.VMEM((2, rows, G * HD), BF),
            pltpu.VMEM((nzh, 2, w.shape[0], width), BF),
            pltpu.VMEM((rows, width), BF),
            pltpu.VMEM((2, half, width), F32),
            pltpu.VMEM((rows, width), F32),
            piece, piece, piece, piece, piece, piece,
            pltpu.VMEM((rows, width), BF),
            dma((4,)), dma((ny, 2, 2)), dma((ny, 2, 2)),
            dma(()), dma(()), dma((2,)), dma((2,)),
            dma((nzh,)), dma((nzh,)), dma((nzh,)),
            dma(()), dma(()),
            dma((2, PARTS)), dma((2, PARTS)), dma((2, PARTS)), dma((2, PARTS)), dma((2, PARTS)), dma((2, PARTS)),
            dma((2, PARTS)), dma((2, PARTS)),
        ],
        compiler_params=pltpu.CompilerParams(
            collective_id=0, has_side_effects=True, vmem_limit_bytes=64 * 1024 * 1024 - 70000
        ),
    )(row_offsets, q, k, v, res, w)
    return out[None]


def solution(mesh):
    placed = (
        P("section"),
        P("section", "ctx", "tp"),
        P("section", "ctx", "tp"),
        P("section", "ctx", "tp"),
        P("section", "ctx", "tp"),
        P("section", "tp", None),
    )
    ny, nzh, nx = mesh.shape["ctx"] // 2, mesh.shape["tp"] // 2, mesh.shape["section"]
    return jax.shard_map(
        functools.partial(on_device, ny, nzh, nx),
        mesh=mesh, in_specs=placed, out_specs=P("section", "ctx", "tp"), check_vma=False,
    )
```

time: 90.5 us -> 83.2 us (0.919)
  local copies, waits for them, and re-layouts: 6.8 us -> 1.6 us
  Pallas kernels: 82.7 us -> 80.8 us
    unnamed x11 -> x1, local copies, waits for them, and re-layouts: 6.8 us -> 1.6 us
    pallas_call x1, Pallas kernels: 82.7 us -> 80.8 us  [on_device(): pl.pallas_call(functools.partial(kernel, ny, nzh, nx), out_shape=jax.Shap...]
where the time goes in v1:
time: 83.2 us; the launch traced here: 83 us
  Pallas kernels  80.8 us (97%)
  local copies, waits for them, and re-layouts  1.6 us (2%)
    pallas_call x1, Pallas kernels, on_device(): pl.pallas_call(functools.partial(kernel, ny, nzh, nx), out_shape=jax.Shap...  80.8 us

profile of v1, /device:TPU:1, one launch (start us, length us, event | category | flops | bytes accessed | tf_op | source)
XLA Modules:
  0.0 83.0 jit_solution(6924789353062691272)
XLA Ops:
  0.7 80.8 %shard_map.64 = bf16[128,640]{1,0:T(8,128)(2,1)} custom-call(s32[1]{0:T(128)S(6)} %copy.8.off_ref, bf16[128,512]{1,0:T(8,128)(2,1)} %bitcast.11, bf16[640,128]{1,0:T(8,128)(2,1)} %bitcast.8, bf16[640,128]{1,0:T(8,128)(2,1)} %bitcast.9, bf16[128,640]{1,0:T(8,128)(2,1)} %bitcast.10, bf16[512,5120]{1,0:T(8,128)(2,1)} %bitcast.6), custom_call_target="tpu_custom_call" | custom-call | tf_op jit(solution)/shard_map/pallas_call | solution.py:310
  81.4 1.6 %copy.9 = bf16[1,128,640]{2,1,0:T(8,128)(2,1)} copy(bf16[1,128,640]{2,1,0:T(8,128)(2,1)} %bitcast.7) | data formatting | bytes 327680

commit v2 on v1

--- a/solution.py
+++ b/solution.py
@@ -20,10 +20,10 @@
 def kernel(
     ny, nzh, nx,
     off_ref, q_ref, k_ref, v_ref, res_ref, w_ref, o_ref,
-    kb, vb, qin, qs, m_ref, l_ref, acc, snd, rcv, att, wbuf, resv, keep, base,
-    far_s, far_r, near_s, near_r, mix_s, mix_r, fin,
+    kb, vb, vt, qin, qs, m_ref, l_ref, acc, snd, rcv, att, wbuf, resv, keep,
+    far_s, far_r, near_s, near_r, mix_s, mix_r, own_s, own_r, fin,
     loc, kv_s, kv_r, q_s, q_r, a_s, a_r, w_l, w_s, w_r, t_s, t_r,
-    far_ss, far_rs, near_ss, near_rs, mix_ss, mix_rs, x_s, x_r,
+    far_ss, far_rs, near_ss, near_rs, mix_ss, mix_rs, own_ss, own_rs, r_s, r_r, o_l,
 ):
     rows = q_ref.shape[0]
     klen = k_ref.shape[0]
@@ -50,6 +50,8 @@
     zring = (zh_next, zh_prev)
     x_next = {"section": (x + 1) % nx}
     x_prev = {"section": (x + nx - 1) % nx}
+    landing = tuple({**x_next, **z} for z in zring)
+    leaving = tuple({**x_prev, **z} for z in zring)
 
     def remote(src, dst, s, r, where):
         return pltpu.make_async_remote_copy(
@@ -62,7 +64,6 @@
     local_k = pltpu.make_async_copy(k_ref, kb.at[0], loc.at[0])
     local_v = pltpu.make_async_copy(v_ref, vb.at[0], loc.at[1])
     local_q = pltpu.make_async_copy(q_ref, qin.at[0], loc.at[2])
-    local_r = pltpu.make_async_copy(res_ref, resv, loc.at[3])
     local_w = [
         pltpu.make_async_copy(w_ref.at[:, wcols(b, co)], wbuf.at[b, co], w_l.at[b]) for b in range(nzh)
     ]
@@ -71,7 +72,7 @@
     local_v.start()
 
     barrier = pltpu.get_barrier_semaphore()
-    greet = (y_next, y_prev, z_mate, core_mate, zh_next, zh_prev, x_next, x_prev)
+    greet = (y_next, y_prev, z_mate, core_mate, zh_next, zh_prev, x_next, x_prev) + landing + leaving
     for where in greet:
         pl.semaphore_signal(barrier, inc=1, device_id=where, device_id_type=MESH)
     pl.semaphore_wait(barrier, len(greet))
@@ -96,7 +97,8 @@
         c.start()
     for c in local_w:
         c.start()
-    local_r.start()
+    send_r = remote(res_ref, resv, r_s, r_r, x_next)
+    send_r.start()
 
     m_ref[...] = jnp.full(m_ref.shape, NEG, F32)
     l_ref[...] = jnp.zeros(l_ref.shape, F32)
@@ -112,37 +114,33 @@
                 col = (2 * g + h) * HD
                 qs[2 * c + g, h * rows : (h + 1) * rows, :] = qin[c, :, col : col + HD]
 
-    def attend(slot, block, i, first, last):
-        start, size = spans[i]
-
-        def group(g, carry):
-            other = g // 2
+    def turn(slot, start, size):
+        vt[slot, :, start : start + size] = vb[slot, start : start + size, :].T
+
+    def attend(slot, block, start, size, first, last):
+        key_pos = (block * 2 + zl) * klen + start + lax.broadcasted_iota(jnp.int32, (size, two), 0)
+
+        def row_class(other, carry):
             row_pos = offset + (y * 2 + zl + other * (1 - 2 * zl)) * rows + lane_row
-            key_pos = (block * 2 + zl) * klen + start + lax.broadcasted_iota(jnp.int32, (size, two), 0)
-            scores = lax.dot_general(
-                kb[slot, start : start + size, :],
-                qs[g],
-                (((1,), (1,)), ((), ())),
-                preferred_element_type=F32,
-            )
-            scores = jnp.where(key_pos <= row_pos, scores, NEG)
-            top = jnp.max(scores, axis=0, keepdims=True).astype(BF).astype(F32)
-            top_old = m_ref[g]
-            top = jnp.maximum(top, top_old)
-            weights = jnp.exp2((scores - top) * scale)
-            fade = jnp.exp2((top_old - top) * scale)
-            m_ref[g] = top
-            l_ref[g] = l_ref[g] * fade + jnp.sum(weights, axis=0, keepdims=True)
-            mixed = lax.dot_general(
-                vb[slot, start : start + size, :],
-                weights.astype(BF),
-                (((0,), (0,)), ((), ())),
-                preferred_element_type=F32,
-            )
-            acc[g] = acc[g] * fade + mixed
+            visible = key_pos <= row_pos
+            for g in (2 * other, 2 * other + 1):
+                scores = lax.dot_general(
+                    kb[slot, start : start + size, :], qs[g], (((1,), (1,)), ((), ())), preferred_element_type=F32
+                )
+                scores = jnp.where(visible, scores, NEG)
+                top_old = m_ref[g]
+                top = jnp.maximum(jnp.max(scores, axis=0, keepdims=True).astype(BF).astype(F32), top_old)
+                weights = jnp.exp2((scores - top) * scale)
+                fade = jnp.exp2((top_old - top) * scale)
+                m_ref[g] = top
+                l_ref[g] = l_ref[g] * fade + jnp.sum(weights, axis=0, keepdims=True)
+                mixed = jnp.dot(
+                    vt[slot, :, start : start + size], weights.astype(BF), preferred_element_type=F32
+                )
+                acc[g] = acc[g] * fade + mixed
             return carry
 
-        lax.fori_loop(first, last, group, 0)
+        lax.fori_loop(first, last, row_class, 0)
 
     def arrive(slot, i, way, kind):
         return hop((kb, vb)[kind].at[slot], slot, i, way, kind)
@@ -151,40 +149,41 @@
     lay_queries(0)
     local_k.wait()
     local_v.wait()
-    for i in (0, 1):
-        attend(0, y, i, 0, 2)
+    turn(0, 0, klen)
+    attend(0, y, 0, klen, 0, 1)
+
+    def forward(h, i):
+        for kind in (0, 1):
+            for way in (0, 1):
+                slot = 2 * h - 1 + way
+                arrive(slot, i, way, kind).wait_recv()
+                dest = 2 * h + 1 if way == 0 else jnp.minimum(2 * h + 2, ny - 1)
+                onward = hop((kb, vb)[kind].at[slot], dest, i, way, kind)
+                if way == i:
+                    onward.start()
+                else:
+
+                    @pl.when(h < hops - 1)
+                    def _():
+                        onward.start()
 
     def round_trip(h, carry):
-        for i in (0, 1):
-            for kind in (0, 1):
-                for way in (0, 1):
-                    slot = 2 * h - 1 + way
-                    arrive(slot, i, way, kind).wait_recv()
-                    dest = 2 * h + 1 if way == 0 else jnp.minimum(2 * h + 2, ny - 1)
-                    onward = hop((kb, vb)[kind].at[slot], dest, i, way, kind)
-                    if way == i:
-                        onward.start()
-                    else:
-
-                        @pl.when(h < hops - 1)
-                        def _():
-                            onward.start()
-
-            if i == 0:
-
-                @pl.when(h == 1)
-                def _():
-                    send_q.wait_recv()
-                    lay_queries(1)
-                    for j in (0, 1):
-                        attend(0, y, j, 2, 4)
-
-            def each(way, c):
-                block = (y + ny + way * 2 * h - h) % ny
-                attend(2 * h - 1 + way, block, i, 0, 4)
-                return c
-
-            lax.fori_loop(0, 2, each, 0)
+        forward(h, 0)
+
+        @pl.when(h == 1)
+        def _():
+            send_q.wait_recv()
+            lay_queries(1)
+            attend(0, y, 0, klen, 1, 2)
+
+        @pl.when(h > 1)
+        def _():
+            turn(2 * h - 2, 0, klen)
+            attend(2 * h - 2, (y + h - 1) % ny, 0, klen, 0, 2)
+
+        forward(h, 1)
+        turn(2 * h - 1, 0, klen)
+        attend(2 * h - 1, (y + ny - h) % ny, 0, klen, 0, 2)
         return carry
 
     lax.fori_loop(1, hops, round_trip, 0)
@@ -193,10 +192,14 @@
     far_block = (y + hops) % ny
     for kind in (0, 1):
         arrive(last, 0, 0, kind).wait_recv()
-    attend(last, far_block, 0, 0, 4)
+    turn(last - 1, 0, klen)
+    attend(last - 1, (y + hops - 1) % ny, 0, klen, 0, 2)
+    turn(last, 0, cut)
+    attend(last, far_block, 0, cut, 0, 2)
     for kind in (0, 1):
         arrive(last, 1, 1, kind).wait_recv()
-    attend(last, far_block, 1, 2, 4)
+    turn(last, cut, klen - cut)
+    attend(last, far_block, cut, klen - cut, 1, 2)
     send_a = [remote(snd.at[g], rcv.at[g], a_s.at[g], a_r.at[g], z_mate) for g in (0, 1)]
     for g in (0, 1):
         snd[g, 0:HD, :] = acc[2 + g].astype(BF)
@@ -209,7 +212,7 @@
         )
         snd[g, HD:, :] = packed.astype(BF)
         send_a[g].start()
-    attend(last, far_block, 1, 0, 2)
+    attend(last, far_block, cut, klen - cut, 0, 1)
     for g in (0, 1):
         send_a[g].wait_recv()
         stats = rcv[g, HD:, :].astype(F32)
@@ -230,7 +233,6 @@
         c.wait()
     for c in send_w:
         c.wait_recv()
-    local_r.wait()
     send_t.wait_recv()
 
     def product(away):
@@ -242,39 +244,44 @@
         return slice(i * half + j * part, i * half + (j + 1) * part)
 
     far_cp = [[remote(far_s.at[i, j], far_r.at[i, j], far_ss.at[i, j], far_rs.at[i, j], zring[i]) for j in range(PARTS)] for i in (0, 1)]
-    near_cp = [[remote(near_s.at[i, j], near_r.at[i, j], near_ss.at[i, j], near_rs.at[i, j], zring[i]) for j in range(PARTS)] for i in (0, 1)]
-    mix_cp = [[remote(mix_s.at[i, j], mix_r.at[i, j], mix_ss.at[i, j], mix_rs.at[i, j], zring[i]) for j in range(PARTS)] for i in (0, 1)]
-    fin_cp = [
-        [remote(fin.at[span(i, j)], o_ref.at[span(i, j)], x_s.at[i, j], x_r.at[i, j], x_next) for j in range(PARTS)]
-        for i in (0, 1)
-    ]
+    near_cp = [[remote(near_s.at[i, j], near_r.at[i, j], near_ss.at[i, j], near_rs.at[i, j], landing[i]) for j in range(PARTS)] for i in (0, 1)]
+    mix_cp = [[remote(mix_s.at[i, j], mix_r.at[i, j], mix_ss.at[i, j], mix_rs.at[i, j], landing[i]) for j in range(PARTS)] for i in (0, 1)]
+    own_cp = [[remote(own_s.at[i, j], own_r.at[i, j], own_ss.at[i, j], own_rs.at[i, j], x_next) for j in range(PARTS)] for i in (0, 1)]
+    out_cp = [[pltpu.make_async_copy(fin.at[span(i, j)], o_ref.at[span(i, j)], o_l.at[i, j]) for j in range(PARTS)] for i in (0, 1)]
 
     opposite = product(2)
     for j in range(PARTS):
         for i in (0, 1):
             far_s[i, j] = opposite[span(i, j)].astype(BF)
             far_cp[i][j].start()
+    own = product(0)
+    for j in range(PARTS):
+        for i in (0, 1):
+            own_s[i, j] = own[span(i, j)].astype(BF)
+            own_cp[i][j].start()
     for i in (0, 1):
         out = product(1 if i == 0 else nzh - 1)
         keep[i] = out[i * half : (i + 1) * half]
         for j in range(PARTS):
             near_s[i, j] = out[span(1 - i, j)].astype(BF)
             near_cp[i][j].start()
-    base[...] = product(0) + resv[...].astype(F32)
     for j in range(PARTS):
         for i in (0, 1):
             far_cp[i][j].wait_recv()
             mix_s[i, j] = (keep[i, j * part : (j + 1) * part] + far_r[i, j].astype(F32)).astype(BF)
             mix_cp[i][j].start()
+    send_r.wait_recv()
     for j in range(PARTS):
         for i in (0, 1):
+            own_cp[i][j].wait_recv()
             near_cp[1 - i][j].wait_recv()
             mix_cp[i][j].wait_recv()
-            summed = base[span(i, j)] + near_r[1 - i, j].astype(F32) + mix_r[i, j].astype(F32)
-            fin[span(i, j)] = summed.astype(BF)
-            fin_cp[i][j].start()
+            summed = own_r[i, j].astype(F32) + near_r[1 - i, j].astype(F32) + mix_r[i, j].astype(F32)
+            fin[span(i, j)] = (resv[span(i, j)].astype(F32) + summed).astype(BF)
+            out_cp[i][j].start()
 
     send_q.wait_send()
+    send_r.wait_send()
     for c in send_w:
         c.wait_send()
     send_t.wait_send()
@@ -291,12 +298,10 @@
     for i in (0, 1):
         for j in range(PARTS):
             far_cp[i][j].wait_send()
+            own_cp[i][j].wait_send()
             near_cp[i][j].wait_send()
             mix_cp[i][j].wait_send()
-    for i in (0, 1):
-        for j in range(PARTS):
-            fin_cp[i][j].wait_send()
-            fin_cp[i][j].wait_recv()
+            out_cp[i][j].wait()
 
 
 def on_device(ny, nzh, nx, row_offsets, queries, cache_keys, cache_values, residual, out_weight):
@@ -315,6 +320,7 @@
         scratch_shapes=[
             pltpu.VMEM((ny, klen, HD), BF),
             pltpu.VMEM((ny, klen, HD), BF),
+            pltpu.VMEM((ny, HD, klen), BF),
             pltpu.VMEM((2, rows, G * HD), BF),
             pltpu.VMEM((4, 2 * rows, HD), BF),
             pltpu.VMEM((4, 1, 2 * HD), F32),
@@ -326,15 +332,14 @@
             pltpu.VMEM((nzh, 2, w.shape[0], width), BF),
             pltpu.VMEM((rows, width), BF),
             pltpu.VMEM((2, half, width), F32),
-            pltpu.VMEM((rows, width), F32),
-            piece, piece, piece, piece, piece, piece,
+            piece, piece, piece, piece, piece, piece, piece, piece,
             pltpu.VMEM((rows, width), BF),
-            dma((4,)), dma((ny, 2, 2)), dma((ny, 2, 2)),
+            dma((3,)), dma((ny, 2, 2)), dma((ny, 2, 2)),
             dma(()), dma(()), dma((2,)), dma((2,)),
             dma((nzh,)), dma((nzh,)), dma((nzh,)),
             dma(()), dma(()),
             dma((2, PARTS)), dma((2, PARTS)), dma((2, PARTS)), dma((2, PARTS)), dma((2, PARTS)), dma((2, PARTS)),
-            dma((2, PARTS)), dma((2, PARTS)),
+            dma((2, PARTS)), dma((2, PARTS)), dma(()), dma(()), dma((2, PARTS)),
         ],
         compiler_params=pltpu.CompilerParams(
             collective_id=0, has_side_effects=True, vmem_limit_bytes=64 * 1024 * 1024 - 70000

time: 83.2 us -> 78 us (0.938)
  Pallas kernels: 80.8 us -> 74.9 us
    pallas_call x1, Pallas kernels: 80.8 us -> 74.9 us  [on_device(): pl.pallas_call(functools.partial(kernel, ny, nzh, nx), out_shape=jax.Shap...]
where the time goes in v2:
time: 78 us; the launch traced here: 77.2 us
  Pallas kernels  74.9 us (96%)
  local copies, waits for them, and re-layouts  1.6 us (2%)
    pallas_call x1, Pallas kernels, on_device(): pl.pallas_call(functools.partial(kernel, ny, nzh, nx), out_shape=jax.Shap...  74.9 us
    unnamed x1, local copies, waits for them, and re-layouts  1.6 us

profile of v2, /device:TPU:1, one launch (start us, length us, event | category | flops | bytes accessed | tf_op | source)
XLA Modules:
  0.0 77.2 jit_solution(13645629326684369320)
XLA Ops:
  0.7 74.9 %shard_map.64 = bf16[128,640]{1,0:T(8,128)(2,1)} custom-call(s32[1]{0:T(128)S(6)} %copy.8.off_ref, bf16[128,512]{1,0:T(8,128)(2,1)} %bitcast.11, bf16[640,128]{1,0:T(8,128)(2,1)} %bitcast.8, bf16[640,128]{1,0:T(8,128)(2,1)} %bitcast.9, bf16[128,640]{1,0:T(8,128)(2,1)} %bitcast.10, bf16[512,5120]{1,0:T(8,128)(2,1)} %bitcast.6), custom_call_target="tpu_custom_call" | custom-call | tf_op jit(solution)/shard_map/pallas_call | solution.py:315
  75.6 1.6 %copy.9 = bf16[1,128,640]{2,1,0:T(8,128)(2,1)} copy(bf16[1,128,640]{2,1,0:T(8,128)(2,1)} %bitcast.7) | data formatting | bytes 327680

commit v3 on v2

--- a/solution.py
+++ b/solution.py
@@ -20,7 +20,7 @@
 def kernel(
     ny, nzh, nx,
     off_ref, q_ref, k_ref, v_ref, res_ref, w_ref, o_ref,
-    kb, vb, vt, qin, qs, m_ref, l_ref, acc, snd, rcv, att, wbuf, resv, keep,
+    kvb, vt, qin, qs, m_ref, l_ref, acc, snd, rcv, att, wbuf, resv, keep,
     far_s, far_r, near_s, near_r, mix_s, mix_r, own_s, own_r, fin,
     loc, kv_s, kv_r, q_s, q_r, a_s, a_r, w_l, w_s, w_r, t_s, t_r,
     far_ss, far_rs, near_ss, near_rs, mix_ss, mix_rs, own_ss, own_rs, r_s, r_r, o_l,
@@ -61,8 +61,8 @@
     def wcols(block, core):
         return pl.ds(pl.multiple_of(block * 2 * width + core * width, width), width)
 
-    local_k = pltpu.make_async_copy(k_ref, kb.at[0], loc.at[0])
-    local_v = pltpu.make_async_copy(v_ref, vb.at[0], loc.at[1])
+    local_k = pltpu.make_async_copy(k_ref, kvb.at[0, 0], loc.at[0])
+    local_v = pltpu.make_async_copy(v_ref, kvb.at[0, 1], loc.at[1])
     local_q = pltpu.make_async_copy(q_ref, qin.at[0], loc.at[2])
     local_w = [
         pltpu.make_async_copy(w_ref.at[:, wcols(b, co)], wbuf.at[b, co], w_l.at[b]) for b in range(nzh)
@@ -79,7 +79,7 @@
 
     def hop(src, slot, i, way, kind):
         at = pl.ds(*spans[i])
-        dst = (kb, vb)[kind].at[slot, at]
+        dst = kvb.at[slot, kind, at]
         return remote(src.at[at], dst, kv_s.at[slot, i, kind], kv_r.at[slot, i, kind], ring[way])
 
     send_q = remote(q_ref, qin.at[1], q_s, q_r, z_mate)
@@ -115,7 +115,7 @@
                 qs[2 * c + g, h * rows : (h + 1) * rows, :] = qin[c, :, col : col + HD]
 
     def turn(slot, start, size):
-        vt[slot, :, start : start + size] = vb[slot, start : start + size, :].T
+        vt[slot, :, start : start + size] = kvb[slot, 1, start : start + size, :].T
 
     def attend(slot, block, start, size, first, last):
         key_pos = (block * 2 + zl) * klen + start + lax.broadcasted_iota(jnp.int32, (size, two), 0)
@@ -125,7 +125,7 @@
             visible = key_pos <= row_pos
             for g in (2 * other, 2 * other + 1):
                 scores = lax.dot_general(
-                    kb[slot, start : start + size, :], qs[g], (((1,), (1,)), ((), ())), preferred_element_type=F32
+                    kvb[slot, 0, start : start + size, :], qs[g], (((1,), (1,)), ((), ())), preferred_element_type=F32
                 )
                 scores = jnp.where(visible, scores, NEG)
                 top_old = m_ref[g]
@@ -143,57 +143,64 @@
         lax.fori_loop(first, last, row_class, 0)
 
     def arrive(slot, i, way, kind):
-        return hop((kb, vb)[kind].at[slot], slot, i, way, kind)
+        return hop(kvb.at[slot, kind], slot, i, way, kind)
 
     local_q.wait()
     lay_queries(0)
     local_k.wait()
     local_v.wait()
     turn(0, 0, klen)
-    attend(0, y, 0, klen, 0, 1)
-
-    def forward(h, i):
-        for kind in (0, 1):
-            for way in (0, 1):
-                slot = 2 * h - 1 + way
-                arrive(slot, i, way, kind).wait_recv()
-                dest = 2 * h + 1 if way == 0 else jnp.minimum(2 * h + 2, ny - 1)
-                onward = hop((kb, vb)[kind].at[slot], dest, i, way, kind)
-                if way == i:
+
+    def forward(h, i, kind):
+        for way in (0, 1):
+            slot = 2 * h - 1 + way
+            arrive(slot, i, way, kind).wait_recv()
+            dest = 2 * h + 1 if way == 0 else jnp.minimum(2 * h + 2, ny - 1)
+            onward = hop(kvb.at[slot, kind], dest, i, way, kind)
+            if way == i:
+                onward.start()
+            else:
+
+                @pl.when(h < hops - 1)
+                def _():
                     onward.start()
-                else:
-
-                    @pl.when(h < hops - 1)
-                    def _():
-                        onward.start()
 
     def round_trip(h, carry):
-        forward(h, 0)
+        forward(h, 0, 0)
+
+        @pl.when(h > 1)
+        def _():
+            attend(2 * h - 3, (y + ny + 1 - h) % ny, 0, klen, 1, 2)
+
+        forward(h, 0, 1)
+
+        @pl.when(h > 1)
+        def _():
+            turn(2 * h - 2, 0, klen)
+
+        attend(2 * h - 2, (y + h - 1) % ny, 0, klen, 0, 1)
+        forward(h, 1, 0)
 
         @pl.when(h == 1)
         def _():
             send_q.wait_recv()
             lay_queries(1)
-            attend(0, y, 0, klen, 1, 2)
-
-        @pl.when(h > 1)
-        def _():
-            turn(2 * h - 2, 0, klen)
-            attend(2 * h - 2, (y + h - 1) % ny, 0, klen, 0, 2)
-
-        forward(h, 1)
+
+        attend(2 * h - 2, (y + h - 1) % ny, 0, klen, 1, 2)
+        forward(h, 1, 1)
         turn(2 * h - 1, 0, klen)
-        attend(2 * h - 1, (y + ny - h) % ny, 0, klen, 0, 2)
+        attend(2 * h - 1, (y + ny - h) % ny, 0, klen, 0, 1)
         return carry
 
     lax.fori_loop(1, hops, round_trip, 0)
 
     last = ny - 1
     far_block = (y + hops) % ny
+    attend(last - 2, (y + ny + 1 - hops) % ny, 0, klen, 1, 2)
+    turn(last - 1, 0, klen)
+    attend(last - 1, (y + hops - 1) % ny, 0, klen, 0, 2)
     for kind in (0, 1):
         arrive(last, 0, 0, kind).wait_recv()
-    turn(last - 1, 0, klen)
-    attend(last - 1, (y + hops - 1) % ny, 0, klen, 0, 2)
     turn(last, 0, cut)
     attend(last, far_block, 0, cut, 0, 2)
     for kind in (0, 1):
@@ -233,12 +240,15 @@
         c.wait()
     for c in send_w:
         c.wait_recv()
+
+    def share(core, away):
+        return jnp.dot(att[core], wbuf[(zh + away) % nzh, core], preferred_element_type=F32)
+
+    first_half = share(co, 2)
     send_t.wait_recv()
 
     def product(away):
-        dest = (zh + away) % nzh
-        out = jnp.dot(att[0], wbuf[dest, 0], preferred_element_type=F32)
-        return out + jnp.dot(att[1], wbuf[dest, 1], preferred_element_type=F32)
+        return share(0, away) + share(1, away)
 
     def span(i, j):
         return slice(i * half + j * part, i * half + (j + 1) * part)
@@ -249,7 +259,7 @@
     own_cp = [[remote(own_s.at[i, j], own_r.at[i, j], own_ss.at[i, j], own_rs.at[i, j], x_next) for j in range(PARTS)] for i in (0, 1)]
     out_cp = [[pltpu.make_async_copy(fin.at[span(i, j)], o_ref.at[span(i, j)], o_l.at[i, j]) for j in range(PARTS)] for i in (0, 1)]
 
-    opposite = product(2)
+    opposite = first_half + share(1 - co, 2)
     for j in range(PARTS):
         for i in (0, 1):
             far_s[i, j] = opposite[span(i, j)].astype(BF)
@@ -318,8 +328,7 @@
         in_specs=[pl.BlockSpec(memory_space=pltpu.SMEM)] + [any_spec] * 5,
         out_specs=any_spec,
         scratch_shapes=[
-            pltpu.VMEM((ny, klen, HD), BF),
-            pltpu.VMEM((ny, klen, HD), BF),
+            pltpu.VMEM((ny, 2, klen, HD), BF),
             pltpu.VMEM((ny, HD, klen), BF),
             pltpu.VMEM((2, rows, G * HD), BF),
             pltpu.VMEM((4, 2 * rows, HD), BF),

time: 78 us -> 77.2 us (0.990)
  Pallas kernels: 74.9 us -> 74.1 us
    pallas_call x1, Pallas kernels: 74.9 us -> 74.1 us  [on_device(): pl.pallas_call(functools.partial(kernel, ny, nzh, nx), out_shape=jax.Shap...]
where the time goes in v3:
time: 77.2 us; the launch traced here: 76.3 us
  Pallas kernels  74.1 us (96%)
  local copies, waits for them, and re-layouts  1.6 us (2%)
    pallas_call x1, Pallas kernels, on_device(): pl.pallas_call(functools.partial(kernel, ny, nzh, nx), out_shape=jax.Shap...  74.1 us
    unnamed x1, local copies, waits for them, and re-layouts  1.6 us

profile of v3, /device:TPU:1, one launch (start us, length us, event | category | flops | bytes accessed | tf_op | source)
XLA Modules:
  0.0 76.3 jit_solution(863195493304051849)
XLA Ops:
  0.7 74.1 %shard_map.64 = bf16[128,640]{1,0:T(8,128)(2,1)} custom-call(s32[1]{0:T(128)S(6)} %copy.8.off_ref, bf16[128,512]{1,0:T(8,128)(2,1)} %bitcast.11, bf16[640,128]{1,0:T(8,128)(2,1)} %bitcast.8, bf16[640,128]{1,0:T(8,128)(2,1)} %bitcast.9, bf16[128,640]{1,0:T(8,128)(2,1)} %bitcast.10, bf16[512,5120]{1,0:T(8,128)(2,1)} %bitcast.6), custom_call_target="tpu_custom_call" | custom-call | tf_op jit(solution)/shard_map/pallas_call | solution.py:325
  74.7 1.6 %copy.9 = bf16[1,128,640]{2,1,0:T(8,128)(2,1)} copy(bf16[1,128,640]{2,1,0:T(8,128)(2,1)} %bitcast.7) | data formatting | bytes 327680

commit v4 on v3

--- a/solution.py
+++ b/solution.py
@@ -44,6 +44,8 @@
     y_prev = {"ctx": ((y + ny - 1) % ny) * 2 + zl}
     ring = (y_next, y_prev)
     z_mate = {"ctx": y * 2 + 1 - zl}
+    cross_to = {"ctx": ((y + ny - 1) % ny) * 2 + 1 - zl}
+    cross_from = {"ctx": ((y + 1) % ny) * 2 + 1 - zl}
     core_mate = {"tp": zh * 2 + 1 - co}
     zh_next = {"tp": ((zh + 1) % nzh) * 2 + co}
     zh_prev = {"tp": ((zh + nzh - 1) % nzh) * 2 + co}
@@ -72,7 +74,7 @@
     local_v.start()
 
     barrier = pltpu.get_barrier_semaphore()
-    greet = (y_next, y_prev, z_mate, core_mate, zh_next, zh_prev, x_next, x_prev) + landing + leaving
+    greet = (y_next, y_prev, z_mate, cross_to, cross_from, core_mate, zh_next, zh_prev, x_next, x_prev) + landing + leaving
     for where in greet:
         pl.semaphore_signal(barrier, inc=1, device_id=where, device_id_type=MESH)
     pl.semaphore_wait(barrier, len(greet))
@@ -114,11 +116,17 @@
                 col = (2 * g + h) * HD
                 qs[2 * c + g, h * rows : (h + 1) * rows, :] = qin[c, :, col : col + HD]
 
+    def cross_hop(kind):
+        at = pl.ds(*spans[1])
+        return remote(
+            kvb.at[ny - 2, kind, at], kvb.at[ny, kind, at], kv_s.at[ny, 1, kind], kv_r.at[ny, 1, kind], cross_to
+        )
+
     def turn(slot, start, size):
         vt[slot, :, start : start + size] = kvb[slot, 1, start : start + size, :].T
 
-    def attend(slot, block, start, size, first, last):
-        key_pos = (block * 2 + zl) * klen + start + lax.broadcasted_iota(jnp.int32, (size, two), 0)
+    def attend(slot, block, start, size, first, last, side=0):
+        key_pos = (block * 2 + zl + side * (1 - 2 * zl)) * klen + start + lax.broadcasted_iota(jnp.int32, (size, two), 0)
 
         def row_class(other, carry):
             row_pos = offset + (y * 2 + zl + other * (1 - 2 * zl)) * rows + lane_row
@@ -159,6 +167,12 @@
             onward = hop(kvb.at[slot, kind], dest, i, way, kind)
             if way == i:
                 onward.start()
+                if way == 1:
+
+                    @pl.when(h == hops - 1)
+                    def _():
+                        cross_hop(kind).start()
+
             else:
 
                 @pl.when(h < hops - 1)
@@ -203,10 +217,6 @@
         arrive(last, 0, 0, kind).wait_recv()
     turn(last, 0, cut)
     attend(last, far_block, 0, cut, 0, 2)
-    for kind in (0, 1):
-        arrive(last, 1, 1, kind).wait_recv()
-    turn(last, cut, klen - cut)
-    attend(last, far_block, cut, klen - cut, 1, 2)
     send_a = [remote(snd.at[g], rcv.at[g], a_s.at[g], a_r.at[g], z_mate) for g in (0, 1)]
     for g in (0, 1):
         snd[g, 0:HD, :] = acc[2 + g].astype(BF)
@@ -219,7 +229,14 @@
         )
         snd[g, HD:, :] = packed.astype(BF)
         send_a[g].start()
+    for kind in (0, 1):
+        arrive(last, 1, 1, kind).wait_recv()
+    turn(last, cut, klen - cut)
     attend(last, far_block, cut, klen - cut, 0, 1)
+    for kind in (0, 1):
+        cross_hop(kind).wait_recv()
+    turn(ny, cut, klen - cut)
+    attend(ny, far_block, cut, klen - cut, 0, 1, 1)
     for g in (0, 1):
         send_a[g].wait_recv()
         stats = rcv[g, HD:, :].astype(F32)
@@ -305,6 +322,8 @@
         return carry
 
     lax.fori_loop(1, ny, drain, 0)
+    for kind in (0, 1):
+        cross_hop(kind).wait_send()
     for i in (0, 1):
         for j in range(PARTS):
             far_cp[i][j].wait_send()
@@ -328,8 +347,8 @@
         in_specs=[pl.BlockSpec(memory_space=pltpu.SMEM)] + [any_spec] * 5,
         out_specs=any_spec,
         scratch_shapes=[
-            pltpu.VMEM((ny, 2, klen, HD), BF),
-            pltpu.VMEM((ny, HD, klen), BF),
+            pltpu.VMEM((ny + 1, 2, klen, HD), BF),
+            pltpu.VMEM((ny + 1, HD, klen), BF),
             pltpu.VMEM((2, rows, G * HD), BF),
             pltpu.VMEM((4, 2 * rows, HD), BF),
             pltpu.VMEM((4, 1, 2 * HD), F32),
@@ -343,7 +362,7 @@
             pltpu.VMEM((2, half, width), F32),
             piece, piece, piece, piece, piece, piece, piece, piece,
             pltpu.VMEM((rows, width), BF),
-            dma((3,)), dma((ny, 2, 2)), dma((ny, 2, 2)),
+            dma((3,)), dma((ny + 1, 2, 2)), dma((ny + 1, 2, 2)),
             dma(()), dma(()), dma((2,)), dma((2,)),
             dma((nzh,)), dma((nzh,)), dma((nzh,)),
             dma(()), dma(()),

time: 77.2 us -> 76.6 us (level)
  no operation moved by 1% of the time
where the time goes in v4:
time: 76.6 us; the launch traced here: 75.7 us
  Pallas kernels  73.5 us (96%)
  local copies, waits for them, and re-layouts  1.6 us (2%)
    pallas_call x1, Pallas kernels, on_device(): pl.pallas_call(functools.partial(kernel, ny, nzh, nx), out_shape=jax.Shap...  73.5 us
    unnamed x1, local copies, waits for them, and re-layouts  1.6 us

profile of v4, /device:TPU:1, one launch (start us, length us, event | category | flops | bytes accessed | tf_op | source)
XLA Modules:
  0.0 75.7 jit_solution(6576473074720582780)
XLA Ops:
  0.7 73.5 %shard_map.64 = bf16[128,640]{1,0:T(8,128)(2,1)} custom-call(s32[1]{0:T(128)S(6)} %copy.8.off_ref, bf16[128,512]{1,0:T(8,128)(2,1)} %bitcast.11, bf16[640,128]{1,0:T(8,128)(2,1)} %bitcast.8, bf16[640,128]{1,0:T(8,128)(2,1)} %bitcast.9, bf16[128,640]{1,0:T(8,128)(2,1)} %bitcast.10, bf16[512,5120]{1,0:T(8,128)(2,1)} %bitcast.6), custom_call_target="tpu_custom_call" | custom-call | tf_op jit(solution)/shard_map/pallas_call | solution.py:344
  74.1 1.6 %copy.9 = bf16[1,128,640]{2,1,0:T(8,128)(2,1)} copy(bf16[1,128,640]{2,1,0:T(8,128)(2,1)} %bitcast.7) | data formatting | bytes 327680

commit v5 on v4

--- a/solution.py
+++ b/solution.py
@@ -11,7 +11,7 @@
 G = 4
 NEG = -(2.0**100)
 LOG2E = 1.4426950408889634
-PARTS = 2
+PARTS = 4
 MESH = pl.DeviceIdType.MESH
 BF = jnp.bfloat16
 F32 = jnp.float32
@@ -216,7 +216,7 @@
     for kind in (0, 1):
         arrive(last, 0, 0, kind).wait_recv()
     turn(last, 0, cut)
-    attend(last, far_block, 0, cut, 0, 2)
+    attend(last, far_block, 0, cut, 1, 2)
     send_a = [remote(snd.at[g], rcv.at[g], a_s.at[g], a_r.at[g], z_mate) for g in (0, 1)]
     for g in (0, 1):
         snd[g, 0:HD, :] = acc[2 + g].astype(BF)
@@ -229,6 +229,7 @@
         )
         snd[g, HD:, :] = packed.astype(BF)
         send_a[g].start()
+    attend(last, far_block, 0, cut, 0, 1)
     for kind in (0, 1):
         arrive(last, 1, 1, kind).wait_recv()
     turn(last, cut, klen - cut)

time: 76.6 us -> 75.5 us (0.986)
  no operation moved by 1% of the time
where the time goes in v5:
time: 75.5 us; the launch traced here: 75.3 us
  Pallas kernels  73.1 us (97%)
  local copies, waits for them, and re-layouts  1.6 us (2%)
    pallas_call x1, Pallas kernels, on_device(): pl.pallas_call(functools.partial(kernel, ny, nzh, nx), out_shape=jax.Shap...  73.1 us
    unnamed x1, local copies, waits for them, and re-layouts  1.6 us

profile of v5, /device:TPU:1, one launch (start us, length us, event | category | flops | bytes accessed | tf_op | source)
XLA Modules:
  0.0 75.3 jit_solution(14063094021146311149)
XLA Ops:
  0.7 73.1 %shard_map.64 = bf16[128,640]{1,0:T(8,128)(2,1)} custom-call(s32[1]{0:T(128)S(6)} %copy.8.off_ref, bf16[128,512]{1,0:T(8,128)(2,1)} %bitcast.11, bf16[640,128]{1,0:T(8,128)(2,1)} %bitcast.8, bf16[640,128]{1,0:T(8,128)(2,1)} %bitcast.9, bf16[128,640]{1,0:T(8,128)(2,1)} %bitcast.10, bf16[512,5120]{1,0:T(8,128)(2,1)} %bitcast.6), custom_call_target="tpu_custom_call" | custom-call | tf_op jit(solution)/shard_map/pallas_call | solution.py:345
  73.7 1.6 %copy.9 = bf16[1,128,640]{2,1,0:T(8,128)(2,1)} copy(bf16[1,128,640]{2,1,0:T(8,128)(2,1)} %bitcast.7) | data formatting | bytes 327680
